TPU v7x, 256 devices: a whole 4x4x8 slice. The times are simulated.
256 devices in a mesh: gx: 16 (over z_hi, y, core), gy: 16 (over x, z_lo).
Axes of the slice: x: 4, y: 4, z: 8 (z_hi: 2, z_lo: 4; z = z_hi * 4 + z_lo), core: 2. Of those that a mesh axis runs over, the one named last changes fastest.
Arguments:
- radiation: float32 [2, 4, 8, 256, 2048], P(None, None, None, 'gx', 'gy'), may hold values from -4 to 4, as said below
- ion_fraction: float32 [8, 256, 2048], P(None, 'gx', 'gy'), may hold values from 0.05 to 0.95
- density: float32 [8, 256, 2048], P(None, 'gx', 'gy'), may hold values from 0.1 to 10
- star_lum: float32 [16, 16, 2, 256], P('gx', 'gy'), may hold values from 0.1 to 10
- star_cell: int32 [16, 16, 3, 256], P('gx', 'gy'), may hold values from 0 to 127, as said below
- star_offset: float32 [16, 16, 3, 256], P('gx', 'gy'), may hold values from 0 to 1
- star_count: int32 [16, 16], P('gx', 'gy'), may hold values from 1 to 256, as said below
Outputs:
- radiation_out: float32 [2, 4, 8, 256, 2048], P(None, None, None, 'gx', 'gy')
- ion_out: float32 [8, 256, 2048], P(None, 'gx', 'gy')
Inputs may be any that keep to these rules, and one draw needn't show every extreme that they name: `star_cell`: per slot: row 0 is the x corner within the tile, 0 to 15; row 1 the y corner, 0 to 127; row 2 the z corner, 0 to 7. `star_count`: some tile has all 256 slots live in every draw. `radiation`: N is positive and |F| < N in every cell.
All inputs are finite; a program needn't handle non-finite values.
Results may differ from a plain program's by a relative error of at most 0.0001.
Values sent between devices are 32-bit elements; how exact they have to be, the bound alone decides.
A program may use at most 64 MiB of HBM per device.

v0:
```python
import functools

import jax
import jax.numpy as jnp
from jax import lax
from jax.experimental import pallas as pl
from jax.experimental.pallas import tpu as pltpu
from jax.sharding import PartitionSpec as P

SUBSTEPS = 4
CHEM_ITERS = 3
DT = 0.3
ALPHA = 0.4
SIGMA = (1.5, 0.5)

MESH = pl.DeviceIdType.MESH
F32 = jnp.float32

ROWS, DEPTH, LANES = 16, 8, 128
HALO = SUBSTEPS
FIELDS = 8
ION, DENS, ARRAYS = 8, 9, 10
STRIP, SLOTS = 24, 5
STRIP_ROW = ROWS + 2 * HALO + 1
TOTAL_ROWS = STRIP_ROW + SLOTS + 1
DIRS = ((1, 1), (1, -1), (-1, 1), (-1, -1), (0, 1), (0, -1), (1, 0), (-1, 0))
SELF_COEF = (1.0 - 3.0 * DT) / (0.5 * DT)


def lane_roll(value, shift):
    if isinstance(shift, int):
        shift = shift % LANES
        return value if shift == 0 else pltpu.roll(value, shift, 1)
    return pltpu.roll(value, lax.rem(shift + LANES, LANES), 1)


def fluxes(u):
    n, fx, fy, fz = u
    n2 = n * n
    f2 = fx * fx + fy * fy + fz * fz
    q = jnp.sqrt(4.0 * n2 - 3.0 * jnp.minimum(f2, n2))
    h = 3.0 / (2.0 * n + q)
    diag = (q - n) * (1.0 / 3.0)
    gx, gy, gz = h * fx, h * fy, h * fz
    pxy, pxz, pyz = gx * fy, gx * fz, gy * fz
    flux_x = (fx, gx * fx + diag, pxy, pxz)
    flux_y = (fy, pxy, gy * fy + diag, pyz)
    flux_z = (fz, pxz, pyz, gz * fz + diag)
    here = []
    for c in range(4):
        side = lane_roll(u[c] - flux_y[c], -1) + lane_roll(u[c] + flux_y[c], 1)
        side = side + pltpu.roll(u[c] - flux_z[c], DEPTH - 1, 0) + pltpu.roll(u[c] + flux_z[c], 1, 0)
        here.append(SELF_COEF * u[c] + side)
    to_lower = [u[c] - flux_x[c] for c in range(4)]
    to_upper = [u[c] + flux_x[c] for c in range(4)]
    return here, to_lower, to_upper


def photochemistry(n1, n2, x0, dens):
    dn = DT * dens
    rec = ALPHA * dn
    m1, m2 = (DT * SIGMA[0]) * n1, (DT * SIGMA[1]) * n2
    x = x0
    for step in range(CHEM_ITERS):
        u = dn * (1.0 - x)
        d1, d2 = 1.0 + SIGMA[0] * u, 1.0 + SIGMA[1] * u
        both = d1 * d2
        gamma = m1 * d2 + m2 * d1
        top = x0 * both + gamma
        bottom = both * (1.0 + rec * x) + gamma
        if step < CHEM_ITERS - 1:
            x = top / bottom
        else:
            inverse = 1.0 / (both * bottom)
            x = top * (both * inverse)
            per_both = bottom * inverse
    return d2 * per_both, d1 * per_both, x


def kernel(
    rad_hbm, ion_hbm, dens_hbm, lum_hbm, cell_hbm, offset_hbm, count_hbm, rad_out, ion_out,
    raw, lum, cell, offset, count, own, own_e, ions, flux_buf, strips, strips_e, final,
    y_send, d_send, ex_send, ey_send, ed_send, x_recv, y_recv, d_recv, ex_recv, ey_recv, ed_recv, raw_out,
    in_sem, out_sem, s_send, s_recv, e_send, e_recv,
):
    nx, ny = lax.axis_size("gx"), lax.axis_size("gy")
    me_x, me_y = lax.axis_index("gx"), lax.axis_index("gy")

    def device(direction):
        dx, dy = direction
        return (lax.rem(me_x + dx + nx, nx), lax.rem(me_y + dy + ny, ny))

    copies_in = [
        pltpu.make_async_copy(src, dst, in_sem.at[i])
        for i, (src, dst) in enumerate(
            (
                (rad_hbm, raw.at[pl.ds(0, FIELDS)]),
                (ion_hbm, raw.at[ION]),
                (dens_hbm, raw.at[DENS]),
                (lum_hbm, lum),
                (cell_hbm, cell),
                (offset_hbm, offset),
                (count_hbm, count),
            )
        )
    ]
    for copy in copies_in:
        copy.start()
    barrier = pltpu.get_barrier_semaphore()
    for direction in DIRS:
        pl.semaphore_signal(barrier, inc=1, device_id=device(direction), device_id_type=MESH)

    lane = lax.broadcasted_iota(jnp.int32, (DEPTH, LANES), 1)
    slot_col = lax.rem(lane, STRIP)
    zeros = jnp.zeros((DEPTH, LANES), F32)

    def between(position, low, width):
        return (position >= low) & (position < low + width)

    def send(src, dst, sems, index, direction):
        copy = pltpu.make_async_remote_copy(
            src_ref=src,
            dst_ref=dst,
            send_sem=sems[0].at[index],
            recv_sem=sems[1].at[index],
            device_id=device(direction),
            device_id_type=MESH,
        )
        copy.start()
        return copy

    for copy in copies_in[:3]:
        copy.wait()

    def unpack(x, packed):
        r = x + HALO
        base = 4 * r + 4 * lax.div(r, SLOTS)
        mask = between(lane, base, 4)
        out = []
        for a in range(ARRAYS):
            row = raw[a, pl.ds(x, DEPTH, stride=ROWS), :]
            own[a, r] = row
            up, down = packed[2 * a], packed[2 * a + 1]
            out.append(jnp.where(mask, lane_roll(row, base + 4), up))
            out.append(jnp.where(mask, lane_roll(row, base), down))
        return tuple(out)

    packed = lax.fori_loop(0, ROWS, unpack, (zeros,) * (2 * ARRAYS))
    for a in range(ARRAYS):
        y_send[0, a] = packed[2 * a]
        y_send[1, a] = packed[2 * a + 1]

    def to_upper_corner(value, first):
        low = lane_roll(value, 24 * first - 76)
        return low

    def corner(value, dx, place, last_row):
        at = STRIP * place
        if dx > 0:
            out = jnp.where(between(lane, at, 16), lane_roll(value, at - 76), 0.0)
            if last_row:
                out = jnp.where(between(lane, at + 16, 4), lane_roll(value, at - 80), out)
            return out
        out = jnp.where(between(lane, at, 4), lane_roll(value, at - 16), 0.0)
        return jnp.where(between(lane, at + 4, 12), lane_roll(value, at - 20), out)

    for i, (dx, dy) in enumerate(DIRS[:4]):
        side = 0 if dy > 0 else 1
        for part in range(2):
            total = zeros
            for place in range(SLOTS):
                total = total + corner(packed[2 * (SLOTS * part + place) + side], dx, place, False)
            d_send[i, part] = total

    pl.semaphore_wait(barrier, len(DIRS))
    state_sems, emit_sems = (s_send, s_recv), (e_send, e_recv)
    state_copies = []
    for i, direction in enumerate(DIRS[:4]):
        state_copies.append(send(d_send.at[i], d_recv.at[i], state_sems, i, direction))
    for i, direction in enumerate(DIRS[4:6]):
        state_copies.append(send(y_send.at[i], y_recv.at[i], state_sems, 4 + i, direction))
    for i, direction in enumerate(DIRS[6:]):
        first = ROWS if i == 0 else HALO
        rows = own.at[:, pl.ds(first, HALO)]
        state_copies.append(send(rows, x_recv.at[i], state_sems, 6 + i, direction))

    for copy in copies_in[3:]:
        copy.wait()
    stars = lum.shape[1]
    live = (lax.broadcasted_iota(jnp.int32, (1, stars), 1) < count[...]).astype(F32)

    def corner_weight(axis, position, upper=None):
        low = cell[axis : axis + 1, :]
        frac = offset[axis : axis + 1, :]
        high = low + 1 if upper is None else upper(low + 1)
        return jnp.where(low == position, 1.0 - frac, 0.0) + jnp.where(high == position, frac, 0.0)

    z_at = lax.broadcasted_iota(jnp.int32, (DEPTH, stars), 0)
    weight_z = corner_weight(2, z_at, lambda c: jnp.where(c >= DEPTH, c - DEPTH, c))
    strength = [weight_z * (lum[g : g + 1, :] * live * DT) for g in range(2)]
    y_at = lax.broadcasted_iota(jnp.int32, (LANES, stars), 0)
    weight_y = corner_weight(1, y_at)
    weight_x = corner_weight(0, y_at)
    over_y = corner_weight(1, jnp.full((1, stars), LANES, jnp.int32))
    spread = []
    for g in range(2):
        for x in range(ROWS + 1):
            spread.append(strength[g] * corner_weight(0, jnp.full((1, stars), x, jnp.int32)))
    contract = functools.partial(
        lax.dot_general,
        dimension_numbers=(((1,), (1,)), ((), ())),
        precision=lax.Precision.HIGHEST,
        preferred_element_type=F32,
    )
    deposit = contract(jnp.concatenate(spread, axis=0), weight_y)
    column = contract(jnp.concatenate([s * over_y for s in strength], axis=0), weight_x)
    for g in range(2):
        for x in range(ROWS + 1):
            at = (g * (ROWS + 1) + x) * DEPTH
            own_e[g, HALO + x] = deposit[at : at + DEPTH]
    for v in range(SLOTS):
        for g in range(2):
            strips_e[g, v] = zeros

    def pack_e(x, carry):
        r = x + HALO
        s = lax.div(r, SLOTS)
        v = r - SLOTS * s
        base = 4 * r + 4 * s
        at = STRIP * s
        mask = between(lane, base, 4)
        out = []
        for g in range(2):
            row = own_e[g, r]
            over = lane_roll(column[g * DEPTH : (g + 1) * DEPTH], LANES - 1 - x)
            moved = jnp.where(lane == LANES - 1, over, lane_roll(row, -1))
            out.append(jnp.where(mask, lane_roll(moved, base + 4), carry[2 * g]))
            out.append(jnp.where(mask, lane_roll(row, base), carry[2 * g + 1]))
            strip = strips_e[g, v]
            strip = jnp.where(between(lane, at + 1, 8), lane_roll(moved, at + 9), strip)
            strips_e[g, v] = jnp.where(between(lane, at + 16, 8), lane_roll(row, at + 16), strip)
        return tuple(out)

    packed_e = lax.fori_loop(0, ROWS + 1, pack_e, (zeros,) * 4)
    for g in range(2):
        ey_send[0, g] = packed_e[2 * g]
        ey_send[1, g] = packed_e[2 * g + 1]
    for i, (dx, dy) in enumerate(DIRS[:4]):
        side = 0 if dy > 0 else 1
        ed_send[i] = corner(packed_e[side], dx, 0, True) + corner(packed_e[2 + side], dx, 1, True)
    for g in range(2):
        for i, (first, moved) in enumerate(((ROWS + 1, 1), (HALO, ROWS + HALO))):
            total = zeros
            for j in range(HALO):
                ex_send[i, g, j] = own_e[g, first + j]
                s, v = divmod(first + j, SLOTS)
                place = (moved + j) % SLOTS
                piece = lane_roll(strips_e[g, v], STRIP * (place - s))
                total = jnp.where(between(lane, STRIP * place, STRIP), piece, total)
            ex_send[i, g, HALO] = total
    emit_copies = []
    for i, direction in enumerate(DIRS[:4]):
        emit_copies.append(send(ed_send.at[i], ed_recv.at[i], emit_sems, i, direction))
    for i, direction in enumerate(DIRS[4:6]):
        emit_copies.append(send(ey_send.at[i], ey_recv.at[i], emit_sems, 4 + i, direction))
    for i, direction in enumerate(DIRS[6:]):
        emit_copies.append(send(ex_send.at[i], ex_recv.at[i], emit_sems, 6 + i, direction))

    def store_flux(k, g, r, u):
        here, to_lower, to_upper = fluxes(u)
        for c in range(4):
            flux_buf[k, g, c, r] = here[c]
            flux_buf[k, g, 4 + c, r] = to_lower[c]
            flux_buf[k, g, 8 + c, r] = to_upper[c]

    def substep(k, r):
        u = []
        for g in range(2):
            for c in range(4):
                total = flux_buf[k - 1, g, c, r] + (flux_buf[k - 1, g, 4 + c, r + 1] + flux_buf[k - 1, g, 8 + c, r - 1])
                u.append((0.5 * DT) * total)
            u[4 * g] = u[4 * g] + own_e[g, r]
        att1, att2, x = photochemistry(u[0], u[4], ions[k - 1, r], ions[SUBSTEPS, r])
        u = [value * (att1 if i < 4 else att2) for i, value in enumerate(u)]
        if k < SUBSTEPS:
            store_flux(k, 0, r, u[:4])
            store_flux(k, 1, r, u[4:])
            ions[k, r] = x
        else:
            for i in range(FIELDS):
                final[i, r] = u[i]
            final[ION, r] = x

    def start_row(i, carry):
        r = HALO + i
        ions[0, r] = own[ION, r]
        ions[SUBSTEPS, r] = own[DENS, r]
        for g in range(2):
            store_flux(0, g, r, [own[4 * g + c, r] for c in range(4)])
        return carry

    lax.fori_loop(0, ROWS, start_row, 0)
    for k in range(1, SUBSTEPS + 1):

        def inner(i, carry, k=k):
            substep(k, HALO + k + 2 * i)
            substep(k, HALO + k + 2 * i + 1)
            return carry

        lax.fori_loop(0, (ROWS - 2 * k) // 2, inner, 0)

    def pack_strip(row, s, old):
        at = STRIP * s
        new = jnp.where(between(lane, at, 8), lane_roll(row, at + 8), old)
        return jnp.where(between(lane, at + 16, 8), lane_roll(row, at + 16), new)

    for a in range(ARRAYS):
        for v in range(SLOTS):
            strips[a, v] = zeros

    def own_strip(i, carry):
        r = HALO + i
        s = lax.div(r, SLOTS)
        v = r - SLOTS * s
        for a in range(ARRAYS):
            strips[a, v] = pack_strip(own[a, r], s, strips[a, v])
        return carry

    lax.fori_loop(0, ROWS, own_strip, 0)

    for i in (6, 7):
        state_copies[i].wait_recv()
        emit_copies[i].wait_recv()

    def start_edge(j, carry):
        for i, r in ((0, j), (1, ROWS + HALO + j)):
            ions[0, r] = x_recv[i, ION, j]
            ions[SUBSTEPS, r] = x_recv[i, DENS, j]
            for g in range(2):
                store_flux(0, g, r, [x_recv[i, 4 * g + c, j] for c in range(4)])
        return carry

    lax.fori_loop(0, HALO, start_edge, 0)
    for g in range(2):
        for j in range(HALO):
            low, high = 1 + j, ROWS + HALO + j
            if j < HALO - 1:
                own_e[g, low] = ex_recv[0, g, j]
            else:
                own_e[g, low] = own_e[g, low] + ex_recv[0, g, j]
            if j == 0:
                own_e[g, high] = own_e[g, high] + ex_recv[1, g, j]
            else:
                own_e[g, high] = ex_recv[1, g, j]
    for k in range(1, SUBSTEPS + 1):

        def edge(i, carry, k=k):
            substep(k, k + i)
            substep(k, ROWS + HALO - k + i)
            return carry

        lax.fori_loop(0, HALO, edge, 0)

    for i in range(6):
        state_copies[i].wait_recv()
        emit_copies[i].wait_recv()

    def unslot(value, place, slot, width):
        return jnp.where(between(lane, STRIP * slot, width), lane_roll(value, STRIP * (slot - place)), 0.0)

    for a in range(ARRAYS):
        part, place = divmod(a, SLOTS)
        edges = []
        for side in range(2):
            edge_cols = y_recv[side, a]
            edge_cols = edge_cols + unslot(d_recv[side, part], place, 0, 16)
            edge_cols = edge_cols + unslot(d_recv[2 + side, part], place, 4, 16)
            edges.append(edge_cols)
        for v in range(SLOTS):
            value = strips[a, v]
            if v < HALO:
                value = pack_strip(x_recv[0, a, v], 0, value)
                value = pack_strip(x_recv[1, a, v], SLOTS - 1, value)
            value = jnp.where(between(slot_col, 12, 4), lane_roll(edges[0], 12 - 4 * v), value)
            value = jnp.where(between(slot_col, 8, 4), lane_roll(edges[1], 8 - 4 * v), value)
            strips[a, v] = value
    for g in range(2):
        edges = []
        for side in range(2):
            edge_cols = ey_recv[side, g]
            edge_cols = edge_cols + unslot(ed_recv[side], g, 0, 20)
            edge_cols = edge_cols + unslot(ed_recv[2 + side], g, 4, 20)
            edges.append(edge_cols)
        for v in range(SLOTS):
            value = strips_e[g, v]
            value = value + jnp.where(between(lane, 0, STRIP), lane_roll(ex_recv[0, g, HALO], -STRIP * v), 0.0)
            value = value + jnp.where(
                between(lane, STRIP * (SLOTS - 1), STRIP),
                lane_roll(ex_recv[1, g, HALO], STRIP * (SLOTS - 1 - v)),
                0.0,
            )
            value = value + jnp.where(between(slot_col, 13, 4), lane_roll(edges[0], 13 - 4 * v), 0.0)
            value = value + jnp.where(between(slot_col, 8, 4), lane_roll(edges[1], 8 - 4 * v), 0.0)
            own_e[g, STRIP_ROW + v] = value

    def wrap_strips(k):
        for g in range(2):
            for c in range(4):
                flux_buf[k, g, 4 + c, STRIP_ROW + SLOTS] = lane_roll(flux_buf[k, g, 4 + c, STRIP_ROW], -STRIP)
                flux_buf[k, g, 8 + c, STRIP_ROW - 1] = lane_roll(flux_buf[k, g, 8 + c, STRIP_ROW + SLOTS - 1], STRIP)

    def start_strip(v, carry):
        ions[0, STRIP_ROW + v] = strips[ION, v]
        ions[SUBSTEPS, STRIP_ROW + v] = strips[DENS, v]
        for g in range(2):
            store_flux(0, g, STRIP_ROW + v, [strips[4 * g + c, v] for c in range(4)])
        return carry

    lax.fori_loop(0, SLOTS, start_strip, 0)
    for k in range(1, SUBSTEPS + 1):
        wrap_strips(k - 1)

        def strip(v, carry, k=k):
            substep(k, STRIP_ROW + v)
            return carry

        lax.fori_loop(0, SLOTS, strip, 0)

    def merge(x, carry):
        r = HALO + x
        s = lax.div(r, SLOTS)
        v = r - SLOTS * s
        for a in range(FIELDS + 1):
            edge_cols = final[a, STRIP_ROW + v]
            value = final[a, r]
            value = jnp.where(lane < HALO, lane_roll(edge_cols, LANES - 16 - STRIP * s), value)
            value = jnp.where(lane >= LANES - HALO, lane_roll(edge_cols, LANES - 8 - STRIP * s), value)
            raw_out[a, pl.ds(x, DEPTH, stride=ROWS), :] = value
        return carry

    lax.fori_loop(0, ROWS, merge, 0)
    copies_out = [
        pltpu.make_async_copy(raw_out.at[pl.ds(0, FIELDS)], rad_out, out_sem.at[0]),
        pltpu.make_async_copy(raw_out.at[ION], ion_out, out_sem.at[1]),
    ]
    for copy in copies_out:
        copy.start()
    for copy in state_copies + emit_copies:
        copy.wait_send()
    for copy in copies_out:
        copy.wait()


def on_device(radiation, ion_fraction, density, star_lum, star_cell, star_offset, star_count):
    groups, comps, depth, rows, lanes = radiation.shape
    assert (groups * comps, depth, rows, lanes) == (FIELDS, DEPTH, ROWS, LANES)
    stars = star_lum.shape[3]
    plane = (depth * rows, lanes)
    vmem = lambda *shape: pltpu.VMEM(shape + (DEPTH, LANES), F32)
    anywhere = pl.BlockSpec(memory_space=pl.ANY)
    rad, ion = pl.pallas_call(
        kernel,
        out_shape=(
            jax.ShapeDtypeStruct((FIELDS,) + plane, F32),
            jax.ShapeDtypeStruct(plane, F32),
        ),
        in_specs=[anywhere] * 7,
        out_specs=(anywhere, anywhere),
        scratch_shapes=[
            pltpu.VMEM((ARRAYS,) + plane, F32),
            pltpu.VMEM((2, stars), F32),
            pltpu.VMEM((3, stars), jnp.int32),
            pltpu.VMEM((3, stars), F32),
            pltpu.VMEM((1, 1), jnp.int32),
            vmem(ARRAYS, ROWS + 2 * HALO),
            vmem(2, TOTAL_ROWS),
            vmem(SUBSTEPS + 1, TOTAL_ROWS),
            vmem(SUBSTEPS, 2, 12, TOTAL_ROWS),
            vmem(ARRAYS, SLOTS),
            vmem(2, SLOTS),
            vmem(FIELDS + 1, TOTAL_ROWS),
            vmem(2, ARRAYS),
            vmem(4, 2),
            vmem(2, 2, HALO + 1),
            vmem(2, 2),
            vmem(4),
            vmem(2, ARRAYS, HALO),
            vmem(2, ARRAYS),
            vmem(4, 2),
            vmem(2, 2, HALO + 1),
            vmem(2, 2),
            vmem(4),
            pltpu.VMEM((FIELDS + 1,) + plane, F32),
            pltpu.SemaphoreType.DMA((7,)),
            pltpu.SemaphoreType.DMA((2,)),
            pltpu.SemaphoreType.DMA((8,)),
            pltpu.SemaphoreType.DMA((8,)),
            pltpu.SemaphoreType.DMA((8,)),
            pltpu.SemaphoreType.DMA((8,)),
        ],
        compiler_params=pltpu.CompilerParams(
            collective_id=0, has_side_effects=True, vmem_limit_bytes=40 * 1024 * 1024
        ),
    )(
        radiation.reshape((FIELDS,) + plane),
        ion_fraction.reshape(plane),
        density.reshape(plane),
        star_lum[0, 0],
        star_cell[0, 0],
        star_offset[0, 0],
        star_count,
    )
    return rad.reshape(radiation.shape), ion.reshape(ion_fraction.shape)


def solution(mesh):
    return jax.shard_map(
        on_device,
        mesh=mesh,
        in_specs=(
            P(None, None, None, "gx", "gy"),
            P(None, "gx", "gy"),
            P(None, "gx", "gy"),
            P("gx", "gy", None, None),
            P("gx", "gy", None, None),
            P("gx", "gy", None, None),
            P("gx", "gy"),
        ),
        out_specs=(P(None, None, None, "gx", "gy"), P(None, "gx", "gy")),
        check_vma=False,
    )
```

profile of v0, /device:TPU:0, one launch (start us, length us, event | category | flops | bytes accessed | tf_op | source)
XLA Modules:
  0.0 37.6 jit_solution(11870305719321288904)
XLA Ops:
  1.3 0.0 copy-start.4
  1.3 0.7 %copy-done.4 = s32[1,1,3,256]{3,1,2,0:T(1,128)S(1)} copy-done((s32[1,1,3,256]{3,1,2,0:T(1,128)S(1)}, s32[1,1,3,256]{3,1,2,0:T(1,128)}, u32[]{:S(2)}) %copy-start.4) | copy-done | bytes 3096
  2.0 0.0 copy-start.5
  2.0 0.7 %copy-done.5 = f32[1,1,3,256]{3,1,2,0:T(1,128)S(1)} copy-done((f32[1,1,3,256]{3,1,2,0:T(1,128)S(1)}, f32[1,1,3,256]{3,1,2,0:T(1,128)}, u32[]{:S(2)}) %copy-start.5) | copy-done | bytes 3096
  2.6 0.0 copy-start.3
  2.7 0.7 %copy-done.3 = f32[1,1,2,256]{3,2,1,0:T(2,128)S(1)} copy-done((f32[1,1,2,256]{3,2,1,0:T(2,128)S(1)}, f32[1,1,2,256]{3,2,1,0:T(2,128)}, u32[]{:S(2)}) %copy-start.3) | copy-done | bytes 2072
  3.3 0.0 copy-start
  3.3 1.0 %copy-done = f32[2,4,8,16,128]{4,3,2,1,0:T(8,128)S(1)} copy-done((f32[2,4,8,16,128]{4,3,2,1,0:T(8,128)S(1)}, f32[2,4,8,16,128]{4,3,2,1,0:T(8,128)}, u32[]{:S(2)}) %copy-start) | copy-done | bytes 524312
  4.4 0.0 copy-start.1
  4.4 0.8 %copy-done.1 = f32[8,16,128]{2,1,0:T(8,128)S(1)} copy-done((f32[8,16,128]{2,1,0:T(8,128)S(1)}, f32[8,16,128]{2,1,0:T(8,128)}, u32[]{:S(2)}) %copy-start.1) | copy-done | bytes 65560
  5.2 0.0 copy-start.2
  5.2 0.8 %copy-done.2 = f32[8,16,128]{2,1,0:T(8,128)S(1)} copy-done((f32[8,16,128]{2,1,0:T(8,128)S(1)}, f32[8,16,128]{2,1,0:T(8,128)}, u32[]{:S(2)}) %copy-start.2) | copy-done | bytes 65560
  6.1 30.1 %shard_map.86 = (f32[8,128,128]{2,1,0:T(8,128)S(1)}, f32[128,128]{1,0:T(8,128)S(1)}) custom-call(f32[8,128,128]{2,1,0:T(8,128)S(1)} %bitcast.12, f32[128,128]{1,0:T(8,128)S(1)} %bitcast.14, f32[128,128]{1,0:T(8,128)S(1)} %bitcast.15, f32[2,256]{1,0:T(2,128)S(1)} %bitcast.19, s32[3,256]{1,0:T(4,128)S(1)} %bitcast.17, f32[3,256]{1,0:T(4,128)S(1)} %bitcast.18, ...), custom_call_target="tpu_custom_call" | custom-call | tf_op jit(solution)/shard_map/pallas_call | solution.py:461
  36.2 0.8 %copy.18 = f32[2,4,8,16,128]{4,3,2,1,0:T(8,128)} copy(f32[2,4,8,16,128]{4,3,2,1,0:T(8,128)S(1)} %bitcast.13) | data formatting | bytes 1048576
  37.0 0.6 %copy.19 = f32[8,16,128]{2,1,0:T(8,128)} copy(f32[8,16,128]{2,1,0:T(8,128)S(1)} %bitcast.16) | data formatting | bytes 131072
  (2 shorter events, 0.0 us)
Async XLA Ops:
  1.3 0.7 %copy-start.4 = (s32[1,1,3,256]{3,1,2,0:T(1,128)S(1)}, s32[1,1,3,256]{3,1,2,0:T(1,128)}, u32[]{:S(2)}) copy-start(s32[1,1,3,256]{3,1,2,0:T(1,128)} %param.11) | copy-start | bytes 9220
  2.0 0.7 %copy-start.5 = (f32[1,1,3,256]{3,1,2,0:T(1,128)S(1)}, f32[1,1,3,256]{3,1,2,0:T(1,128)}, u32[]{:S(2)}) copy-start(f32[1,1,3,256]{3,1,2,0:T(1,128)} %param.12) | copy-start | bytes 9220
  2.6 0.7 %copy-start.3 = (f32[1,1,2,256]{3,2,1,0:T(2,128)S(1)}, f32[1,1,2,256]{3,2,1,0:T(2,128)}, u32[]{:S(2)}) copy-start(f32[1,1,2,256]{3,2,1,0:T(2,128)} %param.10) | copy-start | bytes 6148
  3.3 1.0 %copy-start = (f32[2,4,8,16,128]{4,3,2,1,0:T(8,128)S(1)}, f32[2,4,8,16,128]{4,3,2,1,0:T(8,128)}, u32[]{:S(2)}) copy-start(f32[2,4,8,16,128]{4,3,2,1,0:T(8,128)} %param.7) | copy-start | bytes 1572868
  4.4 0.8 %copy-start.1 = (f32[8,16,128]{2,1,0:T(8,128)S(1)}, f32[8,16,128]{2,1,0:T(8,128)}, u32[]{:S(2)}) copy-start(f32[8,16,128]{2,1,0:T(8,128)} %param.8) | copy-start | bytes 196612
  5.2 0.8 %copy-start.2 = (f32[8,16,128]{2,1,0:T(8,128)S(1)}, f32[8,16,128]{2,1,0:T(8,128)}, u32[]{:S(2)}) copy-start(f32[8,16,128]{2,1,0:T(8,128)} %param.9) | copy-start | bytes 196612
where the time goes:
time: 37.9 us; the launch traced here: 37.6 us
  Pallas kernels  30.1 us (79%)
  local copies, waits for them, and re-layouts  6.18 us (16%)
  between operations  1.3 us (3%)
    pallas_call x1, Pallas kernels, on_device(): pl.pallas_call(kernel, out_shape=(jax.ShapeDtypeStruct((FIELDS,) + plane,...  30.1 us
    unnamed x16, local copies, waits for them, and re-layouts  6.18 us

commit v1 on v0

v1 whole, which is shorter than its diff:
```python
import functools

import jax
import jax.numpy as jnp
from jax import lax
from jax.experimental import pallas as pl
from jax.experimental.pallas import tpu as pltpu
from jax.sharding import PartitionSpec as P

SUBSTEPS = 4
CHEM_ITERS = 3
DT = 0.3
ALPHA = 0.4
SIGMA = (1.5, 0.5)

MESH = pl.DeviceIdType.MESH
F32 = jnp.float32

ROWS, DEPTH, LANES = 16, 8, 128
HALO = SUBSTEPS
FIELDS = 8
ION, DENS, STATE = 8, 9, 10
ARRAYS = STATE + 2
STRIP, SLOTS = 24, 5
STRIP_ROW = ROWS + 2 * HALO + 1
TOTAL_ROWS = STRIP_ROW + SLOTS + 1
DIRS = ((1, 1), (1, -1), (-1, 1), (-1, -1), (0, 1), (0, -1), (1, 0), (-1, 0))
SELF_COEF = (1.0 - 3.0 * DT) / (0.5 * DT)


def lane_roll(value, shift):
    if isinstance(shift, int):
        shift = shift % LANES
        return value if shift == 0 else pltpu.roll(value, shift, 1)
    return pltpu.roll(value, lax.rem(shift + LANES, LANES), 1)


def fluxes(u):
    n, fx, fy, fz = u
    n2 = n * n
    f2 = fx * fx + fy * fy + fz * fz
    q = jnp.sqrt(4.0 * n2 - 3.0 * jnp.minimum(f2, n2))
    h = 3.0 / (2.0 * n + q)
    diag = (q - n) * (1.0 / 3.0)
    gx, gy, gz = h * fx, h * fy, h * fz
    pxy, pxz, pyz = gx * fy, gx * fz, gy * fz
    flux_x = (fx, gx * fx + diag, pxy, pxz)
    flux_y = (fy, pxy, gy * fy + diag, pyz)
    flux_z = (fz, pxz, pyz, gz * fz + diag)
    here = []
    for c in range(4):
        side = lane_roll(u[c] - flux_y[c], -1) + lane_roll(u[c] + flux_y[c], 1)
        side = side + pltpu.roll(u[c] - flux_z[c], DEPTH - 1, 0) + pltpu.roll(u[c] + flux_z[c], 1, 0)
        here.append(SELF_COEF * u[c] + side)
    to_lower = [u[c] - flux_x[c] for c in range(4)]
    to_upper = [u[c] + flux_x[c] for c in range(4)]
    return here, to_lower, to_upper


def photochemistry(n1, n2, x0, dens):
    dn = DT * dens
    rec = ALPHA * dn
    m1, m2 = (DT * SIGMA[0]) * n1, (DT * SIGMA[1]) * n2
    x = x0
    for step in range(CHEM_ITERS):
        u = dn * (1.0 - x)
        d1, d2 = 1.0 + SIGMA[0] * u, 1.0 + SIGMA[1] * u
        both = d1 * d2
        gamma = m1 * d2 + m2 * d1
        top = x0 * both + gamma
        bottom = both * (1.0 + rec * x) + gamma
        if step < CHEM_ITERS - 1:
            x = top / bottom
        else:
            inverse = 1.0 / (both * bottom)
            x = top * (both * inverse)
            per_both = bottom * inverse
    return d2 * per_both, d1 * per_both, x


def kernel(
    rad_hbm, ion_hbm, dens_hbm, lum_hbm, cell_hbm, offset_hbm, count_hbm, rad_out, ion_out,
    raw, lum, cell, offset, count, own, own_e, ions, flux_buf, strips, final,
    y_send, d_send, e_send, x_recv, y_recv, d_recv, e_recv, in_sem, send_sem, recv_sem,
):
    nx, ny = lax.axis_size("gx"), lax.axis_size("gy")
    me_x, me_y = lax.axis_index("gx"), lax.axis_index("gy")

    def device(direction):
        dx, dy = direction
        return (lax.rem(me_x + dx + nx, nx), lax.rem(me_y + dy + ny, ny))

    copies_in = [
        pltpu.make_async_copy(src, dst, in_sem.at[i])
        for i, (src, dst) in enumerate(
            (
                (rad_hbm, raw.at[pl.ds(0, FIELDS)]),
                (ion_hbm, raw.at[ION]),
                (dens_hbm, raw.at[DENS]),
                (lum_hbm, lum),
                (cell_hbm, cell),
                (offset_hbm, offset),
                (count_hbm, count),
            )
        )
    ]
    for copy in copies_in:
        copy.start()
    barrier = pltpu.get_barrier_semaphore()
    for direction in DIRS:
        pl.semaphore_signal(barrier, inc=1, device_id=device(direction), device_id_type=MESH)

    lane = lax.broadcasted_iota(jnp.int32, (DEPTH, LANES), 1)
    slot_col = lax.rem(lane, STRIP)
    zeros = jnp.zeros((DEPTH, LANES), F32)

    def between(position, low, width):
        return (position >= low) & (position < low + width)

    def send(src, dst, index, direction):
        copy = pltpu.make_async_remote_copy(
            src_ref=src,
            dst_ref=dst,
            send_sem=send_sem.at[index],
            recv_sem=recv_sem.at[index],
            device_id=device(direction),
            device_id_type=MESH,
        )
        copy.start()
        return copy

    for copy in copies_in[:3]:
        copy.wait()

    def unpack(x, carry):
        for a in range(STATE):
            own[a, x + HALO] = raw[a, pl.ds(x, DEPTH, stride=ROWS), :]
        return carry

    lax.fori_loop(0, ROWS, unpack, 0)

    for copy in copies_in[3:]:
        copy.wait()
    stars = lum.shape[1]
    live = (lax.broadcasted_iota(jnp.int32, (1, stars), 1) < count[...]).astype(F32)

    def corner_weight(axis, position, wrapped=False):
        low, frac = cell[axis], offset[axis]
        high = low + 1
        if wrapped:
            high = jnp.where(high >= DEPTH, high - DEPTH, high)
        return jnp.where(low == position, 1.0 - frac, 0.0) + jnp.where(high == position, frac, 0.0)

    z_at = lax.broadcasted_iota(jnp.int32, (DEPTH, stars), 0)
    weight_z = corner_weight(2, z_at, True)
    strength = [weight_z * (lum[g : g + 1, :] * live * DT) for g in range(2)]
    y_at = lax.broadcasted_iota(jnp.int32, (LANES, stars), 0)
    weight_y = corner_weight(1, y_at)
    weight_x = corner_weight(0, y_at)
    over_y = corner_weight(1, jnp.full((1, stars), LANES, jnp.int32))
    weight_rows = [corner_weight(0, jnp.full((1, stars), x, jnp.int32)) for x in range(ROWS + 1)]
    spread = [strength[g] * weight_rows[x] for g in range(2) for x in range(ROWS + 1)]
    contract = functools.partial(
        lax.dot_general,
        dimension_numbers=(((1,), (1,)), ((), ())),
        precision=lax.Precision.HIGHEST,
        preferred_element_type=F32,
    )
    deposit = contract(jnp.concatenate(spread, axis=0), weight_y)
    column = contract(jnp.concatenate([s * over_y for s in strength], axis=0), weight_x)
    moved = [[None] * (ROWS + 1) for _ in range(2)]
    for g in range(2):
        for x in range(ROWS + 1):
            at = (g * (ROWS + 1) + x) * DEPTH
            row = deposit[at : at + DEPTH]
            own_e[g, HALO + x] = row
            over = lane_roll(column[g * DEPTH : (g + 1) * DEPTH], LANES - 1 - x)
            moved[g][x] = jnp.where(lane == LANES - 1, over, lane_roll(row, -1))

    def array_row(a, r):
        return own[a, r] if a < STATE else own_e[a - STATE, r]

    packed = {}
    for a in range(ARRAYS):
        for side in range(2):
            total = zeros
            for x in range(ROWS + (a >= STATE)):
                base = 4 * (x + HALO) + 4 * ((x + HALO) // SLOTS)
                if side == 1:
                    piece = lane_roll(array_row(a, x + HALO), base)
                else:
                    row = array_row(a, x + HALO) if a < STATE else moved[a - STATE][x]
                    piece = lane_roll(row, base + 4)
                total = jnp.where(between(lane, base, 4), piece, total)
            packed[a, side] = total
            y_send[side, a] = total

    def corner(value, dx, place, last_row):
        at = STRIP * place
        if dx > 0:
            out = jnp.where(between(lane, at, 16), lane_roll(value, at - 76), 0.0)
            if last_row:
                out = jnp.where(between(lane, at + 16, 4), lane_roll(value, at - 80), out)
            return out
        out = jnp.where(between(lane, at, 4), lane_roll(value, at - 16), 0.0)
        return jnp.where(between(lane, at + 4, 12), lane_roll(value, at - 20), out)

    for i, (dx, dy) in enumerate(DIRS[:4]):
        side = 0 if dy > 0 else 1
        for part in range(3):
            total = zeros
            for place in range(min(SLOTS, ARRAYS - SLOTS * part)):
                a = SLOTS * part + place
                total = total + corner(packed[a, side], dx, place, a >= STATE)
            d_send[i, part] = total

    for g in range(2):
        strip = []
        for v in range(SLOTS):
            total = zeros
            for s in range(SLOTS):
                x, at = SLOTS * s + v - HALO, STRIP * s
                if 0 <= x <= ROWS:
                    total = jnp.where(between(lane, at + 1, 8), lane_roll(moved[g][x], at + 9), total)
                    total = jnp.where(between(lane, at + 16, 8), lane_roll(own_e[g, x + HALO], at + 16), total)
            strip.append(total)
            strips[STATE + g, v] = total
        for i, (first, target) in enumerate(((ROWS + 1, 1), (HALO, ROWS + HALO))):
            total = zeros
            for j in range(HALO):
                e_send[i, g, j] = own_e[g, first + j]
                s, v = divmod(first + j, SLOTS)
                place = (target + j) % SLOTS
                piece = lane_roll(strip[v], STRIP * (place - s))
                total = jnp.where(between(lane, STRIP * place, STRIP), piece, total)
            e_send[i, g, HALO] = total

    pl.semaphore_wait(barrier, len(DIRS))
    copies = []
    for i, direction in enumerate(DIRS[:4]):
        copies.append(send(d_send.at[i], d_recv.at[i], i, direction))
    for i, direction in enumerate(DIRS[4:6]):
        copies.append(send(y_send.at[i], y_recv.at[i], 4 + i, direction))
    for i, direction in enumerate(DIRS[6:]):
        rows = own.at[:, pl.ds(ROWS if i == 0 else HALO, HALO)]
        copies.append(send(rows, x_recv.at[i], 6 + i, direction))
        copies.append(send(e_send.at[i], e_recv.at[i], 8 + i, direction))

    def store_flux(k, g, r, u):
        here, to_lower, to_upper = fluxes(u)
        for c in range(4):
            flux_buf[k, g, c, r] = here[c]
            flux_buf[k, g, 4 + c, r] = to_lower[c]
            flux_buf[k, g, 8 + c, r] = to_upper[c]

    def substep(k, r):
        u = []
        for g in range(2):
            for c in range(4):
                total = flux_buf[k - 1, g, c, r] + (flux_buf[k - 1, g, 4 + c, r + 1] + flux_buf[k - 1, g, 8 + c, r - 1])
                u.append((0.5 * DT) * total)
            u[4 * g] = u[4 * g] + own_e[g, r]
        att1, att2, x = photochemistry(u[0], u[4], ions[k - 1, r], ions[SUBSTEPS, r])
        u = [value * (att1 if i < 4 else att2) for i, value in enumerate(u)]
        if k < SUBSTEPS:
            store_flux(k, 0, r, u[:4])
            store_flux(k, 1, r, u[4:])
            ions[k, r] = x
        else:
            for i in range(FIELDS):
                final[i, r] = u[i]
            final[ION, r] = x

    def start_row(i, carry):
        r = HALO + i
        ions[0, r] = own[ION, r]
        ions[SUBSTEPS, r] = own[DENS, r]
        for g in range(2):
            store_flux(0, g, r, [own[4 * g + c, r] for c in range(4)])
        return carry

    lax.fori_loop(0, ROWS, start_row, 0)
    for k in range(1, SUBSTEPS + 1):

        def inner(i, carry, k=k):
            substep(k, HALO + k + 2 * i)
            substep(k, HALO + k + 2 * i + 1)
            return carry

        lax.fori_loop(0, (ROWS - 2 * k) // 2, inner, 0)

    def pack_strip(row, s, old):
        at = STRIP * s
        new = jnp.where(between(lane, at, 8), lane_roll(row, at + 8), old)
        return jnp.where(between(lane, at + 16, 8), lane_roll(row, at + 16), new)

    for a in range(STATE):
        for v in range(SLOTS):
            total = zeros
            for s in range(SLOTS):
                if HALO <= SLOTS * s + v < HALO + ROWS:
                    total = pack_strip(own[a, SLOTS * s + v], s, total)
            strips[a, v] = total

    for copy in copies[6:]:
        copy.wait_recv()

    def start_edge(j, carry):
        for i, r in ((0, j), (1, ROWS + HALO + j)):
            ions[0, r] = x_recv[i, ION, j]
            ions[SUBSTEPS, r] = x_recv[i, DENS, j]
            for g in range(2):
                store_flux(0, g, r, [x_recv[i, 4 * g + c, j] for c in range(4)])
        return carry

    lax.fori_loop(0, HALO, start_edge, 0)
    for g in range(2):
        for j in range(HALO):
            low, high = 1 + j, ROWS + HALO + j
            if j < HALO - 1:
                own_e[g, low] = e_recv[0, g, j]
            else:
                own_e[g, low] = own_e[g, low] + e_recv[0, g, j]
            if j == 0:
                own_e[g, high] = own_e[g, high] + e_recv[1, g, j]
            else:
                own_e[g, high] = e_recv[1, g, j]
    for k in range(1, SUBSTEPS + 1):

        def edge(i, carry, k=k):
            substep(k, k + i)
            substep(k, ROWS + HALO - k + i)
            return carry

        lax.fori_loop(0, HALO, edge, 0)

    for copy in copies[:6]:
        copy.wait_recv()

    def unslot(value, place, slot, width):
        return jnp.where(between(lane, STRIP * slot, width), lane_roll(value, STRIP * (slot - place)), 0.0)

    for a in range(ARRAYS):
        part, place = divmod(a, SLOTS)
        deposits = a >= STATE
        edges = []
        for side in range(2):
            edge_cols = y_recv[side, a]
            edge_cols = edge_cols + unslot(d_recv[side, part], place, 0, 20 if deposits else 16)
            edge_cols = edge_cols + unslot(d_recv[2 + side, part], place, 4, 16)
            edges.append(edge_cols)
        for v in range(SLOTS):
            value = strips[a, v]
            if deposits:
                g = a - STATE
                last = STRIP * (SLOTS - 1)
                lower, upper = e_recv[0, g, HALO], e_recv[1, g, HALO]
                value = value + jnp.where(lane < STRIP, lane_roll(lower, -STRIP * v), 0.0)
                value = value + jnp.where(between(lane, last, STRIP), lane_roll(upper, last - STRIP * v), 0.0)
                value = value + jnp.where(between(slot_col, 13, 4), lane_roll(edges[0], 13 - 4 * v), 0.0)
                value = value + jnp.where(between(slot_col, 8, 4), lane_roll(edges[1], 8 - 4 * v), 0.0)
                own_e[g, STRIP_ROW + v] = value
                continue
            if v < HALO:
                value = pack_strip(x_recv[0, a, v], 0, value)
                value = pack_strip(x_recv[1, a, v], SLOTS - 1, value)
            value = jnp.where(between(slot_col, 12, 4), lane_roll(edges[0], 12 - 4 * v), value)
            value = jnp.where(between(slot_col, 8, 4), lane_roll(edges[1], 8 - 4 * v), value)
            strips[a, v] = value

    def wrap_strips(k):
        for g in range(2):
            for c in range(4):
                flux_buf[k, g, 4 + c, STRIP_ROW + SLOTS] = lane_roll(flux_buf[k, g, 4 + c, STRIP_ROW], -STRIP)
                flux_buf[k, g, 8 + c, STRIP_ROW - 1] = lane_roll(flux_buf[k, g, 8 + c, STRIP_ROW + SLOTS - 1], STRIP)

    def start_strip(v, carry):
        ions[0, STRIP_ROW + v] = strips[ION, v]
        ions[SUBSTEPS, STRIP_ROW + v] = strips[DENS, v]
        for g in range(2):
            store_flux(0, g, STRIP_ROW + v, [strips[4 * g + c, v] for c in range(4)])
        return carry

    lax.fori_loop(0, SLOTS, start_strip, 0)
    for k in range(1, SUBSTEPS + 1):
        wrap_strips(k - 1)

        for v in range(SLOTS):
            substep(k, STRIP_ROW + v)

    for x in range(ROWS):
        s, v = divmod(x + HALO, SLOTS)
        for a in range(FIELDS + 1):
            edge_cols = final[a, STRIP_ROW + v]
            value = final[a, x + HALO]
            value = jnp.where(lane < HALO, lane_roll(edge_cols, -16 - STRIP * s), value)
            value = jnp.where(lane >= LANES - HALO, lane_roll(edge_cols, -8 - STRIP * s), value)
            if a < FIELDS:
                rad_out[a, pl.ds(x, DEPTH, stride=ROWS), :] = value
            else:
                ion_out[pl.ds(x, DEPTH, stride=ROWS), :] = value
    for copy in copies:
        copy.wait_send()


def on_device(radiation, ion_fraction, density, star_lum, star_cell, star_offset, star_count):
    groups, comps, depth, rows, lanes = radiation.shape
    assert (groups * comps, depth, rows, lanes) == (FIELDS, DEPTH, ROWS, LANES)
    stars = star_lum.shape[3]
    plane = (depth * rows, lanes)
    vmem = lambda *shape: pltpu.VMEM(shape + (DEPTH, LANES), F32)
    hbm = lambda value: pltpu.with_memory_space_constraint(value, pltpu.HBM)
    rad, ion = pl.pallas_call(
        kernel,
        out_shape=(
            jax.ShapeDtypeStruct((FIELDS,) + plane, F32),
            jax.ShapeDtypeStruct(plane, F32),
        ),
        in_specs=[pl.BlockSpec(memory_space=pltpu.HBM)] * 7,
        out_specs=(pl.BlockSpec(memory_space=pltpu.VMEM),) * 2,
        scratch_shapes=[
            pltpu.VMEM((STATE,) + plane, F32),
            pltpu.VMEM((2, stars), F32),
            pltpu.VMEM((3, 1, stars), jnp.int32),
            pltpu.VMEM((3, 1, stars), F32),
            pltpu.VMEM((1, 1), jnp.int32),
            vmem(STATE, ROWS + 2 * HALO),
            vmem(2, TOTAL_ROWS),
            vmem(SUBSTEPS + 1, TOTAL_ROWS),
            vmem(SUBSTEPS, 2, 12, TOTAL_ROWS),
            vmem(ARRAYS, SLOTS),
            vmem(FIELDS + 1, TOTAL_ROWS),
            vmem(2, ARRAYS),
            vmem(4, 3),
            vmem(2, 2, HALO + 1),
            vmem(2, STATE, HALO),
            vmem(2, ARRAYS),
            vmem(4, 3),
            vmem(2, 2, HALO + 1),
            pltpu.SemaphoreType.DMA((7,)),
            pltpu.SemaphoreType.DMA((10,)),
            pltpu.SemaphoreType.DMA((10,)),
        ],
        compiler_params=pltpu.CompilerParams(
            collective_id=0, has_side_effects=True, vmem_limit_bytes=40 * 1024 * 1024
        ),
    )(
        hbm(radiation.reshape((FIELDS,) + plane)),
        hbm(ion_fraction.reshape(plane)),
        hbm(density.reshape(plane)),
        hbm(star_lum[0, 0]),
        hbm(star_cell.reshape(3, 1, stars)),
        hbm(star_offset.reshape(3, 1, stars)),
        star_count,
    )
    return rad.reshape(radiation.shape), ion.reshape(ion_fraction.shape)


def solution(mesh):
    return jax.shard_map(
        on_device,
        mesh=mesh,
        in_specs=(
            P(None, None, None, "gx", "gy"),
            P(None, "gx", "gy"),
            P(None, "gx", "gy"),
            P("gx", "gy", None, None),
            P("gx", "gy", None, None),
            P("gx", "gy", None, None),
            P("gx", "gy"),
        ),
        out_specs=(P(None, None, None, "gx", "gy"), P(None, "gx", "gy")),
        check_vma=False,
    )
```

time: 37.9 us -> 29 us (0.77)
  local copies, waits for them, and re-layouts: 6.18 us -> 1.42 us
  Pallas kernels: 30.1 us -> 26.1 us
    unnamed x16 -> x2, local copies, waits for them, and re-layouts: 6.18 us -> 1.42 us
    pallas_call x1, Pallas kernels: 30.1 us -> 26.1 us  [on_device(): pl.pallas_call(kernel, out_shape=(jax.ShapeDtypeStruct((FIELDS,) + plane,...]
where the time goes in v1:
time: 29 us; the launch traced here: 28.8 us
  Pallas kernels  26.1 us (90%)
  local copies, waits for them, and re-layouts  1.42 us (5%)
  between operations  1.29 us (4%)
    pallas_call x1, Pallas kernels, on_device(): pl.pallas_call(kernel, out_shape=(jax.ShapeDtypeStruct((FIELDS,) + plane,...  26.1 us
    unnamed x2, local copies, waits for them, and re-layouts  1.42 us

profile of v1, /device:TPU:0, one launch (start us, length us, event | category | flops | bytes accessed | tf_op | source)
XLA Modules:
  0.0 28.8 jit_solution(17640794017155477082)
XLA Ops:
  1.3 26.1 %shard_map.86 = (f32[8,128,128]{2,1,0:T(8,128)S(1)}, f32[128,128]{1,0:T(8,128)S(1)}) custom-call(f32[8,128,128]{2,1,0:T(8,128)} %bitcast.10, f32[128,128]{1,0:T(8,128)} %bitcast.11, f32[128,128]{1,0:T(8,128)} %bitcast.12, f32[2,256]{1,0:T(2,128)} %bitcast.15, s32[3,1,256]{2,1,0:T(1,128)} %bitcast.13, f32[3,1,256]{2,1,0:T(1,128)} %bitcast.14, ...), custom_call_target="tpu_custom_call" | custom-call | tf_op jit(solution)/shard_map/pallas_call | solution.py:413
  27.4 0.8 %copy.12 = f32[2,4,8,16,128]{4,3,2,1,0:T(8,128)} copy(f32[2,4,8,16,128]{4,3,2,1,0:T(8,128)S(1)} %bitcast.8) | data formatting | bytes 1048576
  28.2 0.6 %copy.13 = f32[8,16,128]{2,1,0:T(8,128)} copy(f32[8,16,128]{2,1,0:T(8,128)S(1)} %bitcast.9) | data formatting | bytes 131072

commit v2 on v1

--- a/solution.py
+++ b/solution.py
@@ -24,7 +24,7 @@
 STRIP, SLOTS = 24, 5
 STRIP_ROW = ROWS + 2 * HALO + 1
 TOTAL_ROWS = STRIP_ROW + SLOTS + 1
-DIRS = ((1, 1), (1, -1), (-1, 1), (-1, -1), (0, 1), (0, -1), (1, 0), (-1, 0))
+DIRS = ((0, 1), (0, -1), (1, 0), (-1, 0))
 SELF_COEF = (1.0 - 3.0 * DT) / (0.5 * DT)
 
 
@@ -132,12 +132,9 @@
     for copy in copies_in[:3]:
         copy.wait()
 
-    def unpack(x, carry):
+    for x in range(ROWS):
         for a in range(STATE):
             own[a, x + HALO] = raw[a, pl.ds(x, DEPTH, stride=ROWS), :]
-        return carry
-
-    lax.fori_loop(0, ROWS, unpack, 0)
 
     for copy in copies_in[3:]:
         copy.wait()
@@ -180,7 +177,6 @@
     def array_row(a, r):
         return own[a, r] if a < STATE else own_e[a - STATE, r]
 
-    packed = {}
     for a in range(ARRAYS):
         for side in range(2):
             total = zeros
@@ -192,27 +188,7 @@
                     row = array_row(a, x + HALO) if a < STATE else moved[a - STATE][x]
                     piece = lane_roll(row, base + 4)
                 total = jnp.where(between(lane, base, 4), piece, total)
-            packed[a, side] = total
             y_send[side, a] = total
-
-    def corner(value, dx, place, last_row):
-        at = STRIP * place
-        if dx > 0:
-            out = jnp.where(between(lane, at, 16), lane_roll(value, at - 76), 0.0)
-            if last_row:
-                out = jnp.where(between(lane, at + 16, 4), lane_roll(value, at - 80), out)
-            return out
-        out = jnp.where(between(lane, at, 4), lane_roll(value, at - 16), 0.0)
-        return jnp.where(between(lane, at + 4, 12), lane_roll(value, at - 20), out)
-
-    for i, (dx, dy) in enumerate(DIRS[:4]):
-        side = 0 if dy > 0 else 1
-        for part in range(3):
-            total = zeros
-            for place in range(min(SLOTS, ARRAYS - SLOTS * part)):
-                a = SLOTS * part + place
-                total = total + corner(packed[a, side], dx, place, a >= STATE)
-            d_send[i, part] = total
 
     for g in range(2):
         strip = []
@@ -236,15 +212,12 @@
             e_send[i, g, HALO] = total
 
     pl.semaphore_wait(barrier, len(DIRS))
-    copies = []
-    for i, direction in enumerate(DIRS[:4]):
-        copies.append(send(d_send.at[i], d_recv.at[i], i, direction))
-    for i, direction in enumerate(DIRS[4:6]):
-        copies.append(send(y_send.at[i], y_recv.at[i], 4 + i, direction))
-    for i, direction in enumerate(DIRS[6:]):
-        rows = own.at[:, pl.ds(ROWS if i == 0 else HALO, HALO)]
-        copies.append(send(rows, x_recv.at[i], 6 + i, direction))
-        copies.append(send(e_send.at[i], e_recv.at[i], 8 + i, direction))
+    y_copies = [send(y_send.at[i], y_recv.at[i], i, DIRS[i]) for i in range(2)]
+    x_copies = []
+    for i in range(2):
+        rows = own.at[:, pl.ds(HALO if i else ROWS, HALO)]
+        x_copies.append(send(rows, x_recv.at[i], 2 + i, DIRS[2 + i]))
+        x_copies.append(send(e_send.at[i], e_recv.at[i], 4 + i, DIRS[2 + i]))
 
     def store_flux(k, g, r, u):
         here, to_lower, to_upper = fluxes(u)
@@ -271,23 +244,14 @@
                 final[i, r] = u[i]
             final[ION, r] = x
 
-    def start_row(i, carry):
-        r = HALO + i
+    for r in range(HALO, HALO + ROWS):
         ions[0, r] = own[ION, r]
         ions[SUBSTEPS, r] = own[DENS, r]
         for g in range(2):
             store_flux(0, g, r, [own[4 * g + c, r] for c in range(4)])
-        return carry
-
-    lax.fori_loop(0, ROWS, start_row, 0)
     for k in range(1, SUBSTEPS + 1):
-
-        def inner(i, carry, k=k):
-            substep(k, HALO + k + 2 * i)
-            substep(k, HALO + k + 2 * i + 1)
-            return carry
-
-        lax.fori_loop(0, (ROWS - 2 * k) // 2, inner, 0)
+        for r in range(HALO + k, HALO + ROWS - k):
+            substep(k, r)
 
     def pack_strip(row, s, old):
         at = STRIP * s
@@ -302,18 +266,49 @@
                     total = pack_strip(own[a, SLOTS * s + v], s, total)
             strips[a, v] = total
 
-    for copy in copies[6:]:
+    def corner(value, dx, place, last_row):
+        at = STRIP * place
+        if dx > 0:
+            out = jnp.where(between(lane, at, 16), lane_roll(value, at - 76), 0.0)
+            if last_row:
+                out = jnp.where(between(lane, at + 16, 4), lane_roll(value, at - 80), out)
+            return out
+        out = jnp.where(between(lane, at, 4), lane_roll(value, at - 16), 0.0)
+        return jnp.where(between(lane, at + 4, 12), lane_roll(value, at - 20), out)
+
+    for copy in y_copies:
         copy.wait_recv()
-
-    def start_edge(j, carry):
+    for i in range(2):
+        for side in range(2):
+            for part in range(3):
+                total = zeros
+                for place in range(min(SLOTS, ARRAYS - SLOTS * part)):
+                    a = SLOTS * part + place
+                    total = total + corner(y_recv[side, a], 1 if i == 0 else -1, place, a >= STATE)
+                d_send[i, side, part] = total
+    d_copies = [send(d_send.at[i], d_recv.at[i], 6 + i, DIRS[2 + i]) for i in range(2)]
+
+    def add_edges(lower, upper, v, deposits, value, mask):
+        first = 13 if deposits else 12
+        lower_mask, upper_mask = between(slot_col, first, 4), between(slot_col, 8, 4)
+        if mask is not None:
+            lower_mask, upper_mask = lower_mask & mask, upper_mask & mask
+        other = value if deposits else 0.0
+        value = jnp.where(lower_mask, lane_roll(lower, first - 4 * v) + other, value)
+        return jnp.where(upper_mask, lane_roll(upper, 8 - 4 * v) + other, value)
+
+    for a in range(ARRAYS):
+        for v in range(SLOTS):
+            strips[a, v] = add_edges(y_recv[0, a], y_recv[1, a], v, a >= STATE, strips[a, v], None)
+
+    for copy in x_copies:
+        copy.wait_recv()
+    for j in range(HALO):
         for i, r in ((0, j), (1, ROWS + HALO + j)):
             ions[0, r] = x_recv[i, ION, j]
             ions[SUBSTEPS, r] = x_recv[i, DENS, j]
             for g in range(2):
                 store_flux(0, g, r, [x_recv[i, 4 * g + c, j] for c in range(4)])
-        return carry
-
-    lax.fori_loop(0, HALO, start_edge, 0)
     for g in range(2):
         for j in range(HALO):
             low, high = 1 + j, ROWS + HALO + j
@@ -326,15 +321,23 @@
             else:
                 own_e[g, high] = e_recv[1, g, j]
     for k in range(1, SUBSTEPS + 1):
-
-        def edge(i, carry, k=k):
+        for i in range(HALO):
             substep(k, k + i)
             substep(k, ROWS + HALO - k + i)
-            return carry
-
-        lax.fori_loop(0, HALO, edge, 0)
-
-    for copy in copies[:6]:
+
+    outer = (lane < STRIP) | between(lane, STRIP * (SLOTS - 1), STRIP)
+    for a in range(STATE):
+        for v in range(HALO):
+            value = pack_strip(x_recv[0, a, v], 0, strips[a, v])
+            strips[a, v] = pack_strip(x_recv[1, a, v], SLOTS - 1, value)
+    for g in range(2):
+        for v in range(SLOTS):
+            last = STRIP * (SLOTS - 1)
+            value = strips[STATE + g, v]
+            value = value + jnp.where(lane < STRIP, lane_roll(e_recv[0, g, HALO], -STRIP * v), 0.0)
+            piece = lane_roll(e_recv[1, g, HALO], last - STRIP * v)
+            strips[STATE + g, v] = value + jnp.where(between(lane, last, STRIP), piece, 0.0)
+    for copy in d_copies:
         copy.wait_recv()
 
     def unslot(value, place, slot, width):
@@ -345,28 +348,16 @@
         deposits = a >= STATE
         edges = []
         for side in range(2):
-            edge_cols = y_recv[side, a]
-            edge_cols = edge_cols + unslot(d_recv[side, part], place, 0, 20 if deposits else 16)
-            edge_cols = edge_cols + unslot(d_recv[2 + side, part], place, 4, 16)
-            edges.append(edge_cols)
-        for v in range(SLOTS):
-            value = strips[a, v]
+            low = unslot(d_recv[0, side, part], place, 0, 20 if deposits else 16)
+            edges.append(low + unslot(d_recv[1, side, part], place, SLOTS - 1, 16))
+        for v in range(SLOTS):
+            if not deposits and v == SLOTS - 1:
+                continue
+            value = add_edges(edges[0], edges[1], v, deposits, strips[a, v], outer)
             if deposits:
-                g = a - STATE
-                last = STRIP * (SLOTS - 1)
-                lower, upper = e_recv[0, g, HALO], e_recv[1, g, HALO]
-                value = value + jnp.where(lane < STRIP, lane_roll(lower, -STRIP * v), 0.0)
-                value = value + jnp.where(between(lane, last, STRIP), lane_roll(upper, last - STRIP * v), 0.0)
-                value = value + jnp.where(between(slot_col, 13, 4), lane_roll(edges[0], 13 - 4 * v), 0.0)
-                value = value + jnp.where(between(slot_col, 8, 4), lane_roll(edges[1], 8 - 4 * v), 0.0)
-                own_e[g, STRIP_ROW + v] = value
-                continue
-            if v < HALO:
-                value = pack_strip(x_recv[0, a, v], 0, value)
-                value = pack_strip(x_recv[1, a, v], SLOTS - 1, value)
-            value = jnp.where(between(slot_col, 12, 4), lane_roll(edges[0], 12 - 4 * v), value)
-            value = jnp.where(between(slot_col, 8, 4), lane_roll(edges[1], 8 - 4 * v), value)
-            strips[a, v] = value
+                own_e[a - STATE, STRIP_ROW + v] = value
+            else:
+                strips[a, v] = value
 
     def wrap_strips(k):
         for g in range(2):
@@ -374,14 +365,11 @@
                 flux_buf[k, g, 4 + c, STRIP_ROW + SLOTS] = lane_roll(flux_buf[k, g, 4 + c, STRIP_ROW], -STRIP)
                 flux_buf[k, g, 8 + c, STRIP_ROW - 1] = lane_roll(flux_buf[k, g, 8 + c, STRIP_ROW + SLOTS - 1], STRIP)
 
-    def start_strip(v, carry):
+    for v in range(SLOTS):
         ions[0, STRIP_ROW + v] = strips[ION, v]
         ions[SUBSTEPS, STRIP_ROW + v] = strips[DENS, v]
         for g in range(2):
             store_flux(0, g, STRIP_ROW + v, [strips[4 * g + c, v] for c in range(4)])
-        return carry
-
-    lax.fori_loop(0, SLOTS, start_strip, 0)
     for k in range(1, SUBSTEPS + 1):
         wrap_strips(k - 1)
 
@@ -399,7 +387,7 @@
                 rad_out[a, pl.ds(x, DEPTH, stride=ROWS), :] = value
             else:
                 ion_out[pl.ds(x, DEPTH, stride=ROWS), :] = value
-    for copy in copies:
+    for copy in y_copies + x_copies + d_copies:
         copy.wait_send()
 
 
@@ -431,15 +419,15 @@
             vmem(ARRAYS, SLOTS),
             vmem(FIELDS + 1, TOTAL_ROWS),
             vmem(2, ARRAYS),
-            vmem(4, 3),
+            vmem(2, 2, 3),
             vmem(2, 2, HALO + 1),
             vmem(2, STATE, HALO),
             vmem(2, ARRAYS),
-            vmem(4, 3),
+            vmem(2, 2, 3),
             vmem(2, 2, HALO + 1),
             pltpu.SemaphoreType.DMA((7,)),
-            pltpu.SemaphoreType.DMA((10,)),
-            pltpu.SemaphoreType.DMA((10,)),
+            pltpu.SemaphoreType.DMA((8,)),
+            pltpu.SemaphoreType.DMA((8,)),
         ],
         compiler_params=pltpu.CompilerParams(
             collective_id=0, has_side_effects=True, vmem_limit_bytes=40 * 1024 * 1024

time: 29 us -> 25.3 us (0.87)
  Pallas kernels: 26.1 us -> 22.5 us
    pallas_call x1, Pallas kernels: 26.1 us -> 22.5 us  [on_device(): pl.pallas_call(kernel, out_shape=(jax.ShapeDtypeStruct((FIELDS,) + plane,...]
where the time goes in v2:
time: 25.3 us; the launch traced here: 25.2 us
  Pallas kernels  22.5 us (89%)
  local copies, waits for them, and re-layouts  1.42 us (6%)
  between operations  1.29 us (5%)
    pallas_call x1, Pallas kernels, on_device(): pl.pallas_call(kernel, out_shape=(jax.ShapeDtypeStruct((FIELDS,) + plane,...  22.5 us
    unnamed x2, local copies, waits for them, and re-layouts  1.42 us

profile of v2, /device:TPU:0, one launch (start us, length us, event | category | flops | bytes accessed | tf_op | source)
XLA Modules:
  0.0 25.2 jit_solution(17995269602016858345)
XLA Ops:
  1.3 22.5 %shard_map.86 = (f32[8,128,128]{2,1,0:T(8,128)S(1)}, f32[128,128]{1,0:T(8,128)S(1)}) custom-call(f32[8,128,128]{2,1,0:T(8,128)} %bitcast.10, f32[128,128]{1,0:T(8,128)} %bitcast.11, f32[128,128]{1,0:T(8,128)} %bitcast.12, f32[2,256]{1,0:T(2,128)} %bitcast.15, s32[3,1,256]{2,1,0:T(1,128)} %bitcast.13, f32[3,1,256]{2,1,0:T(1,128)} %bitcast.14, ...), custom_call_target="tpu_custom_call" | custom-call | tf_op jit(solution)/shard_map/pallas_call | solution.py:401
  23.8 0.8 %copy.12 = f32[2,4,8,16,128]{4,3,2,1,0:T(8,128)} copy(f32[2,4,8,16,128]{4,3,2,1,0:T(8,128)S(1)} %bitcast.8) | data formatting | bytes 1048576
  24.6 0.6 %copy.13 = f32[8,16,128]{2,1,0:T(8,128)} copy(f32[8,16,128]{2,1,0:T(8,128)S(1)} %bitcast.9) | data formatting | bytes 131072

commit v3 on v2

--- a/solution.py
+++ b/solution.py
@@ -79,9 +79,9 @@
 
 
 def kernel(
-    rad_hbm, ion_hbm, dens_hbm, lum_hbm, cell_hbm, offset_hbm, count_hbm, rad_out, ion_out,
-    raw, lum, cell, offset, count, own, own_e, ions, flux_buf, strips, final,
-    y_send, d_send, e_send, x_recv, y_recv, d_recv, e_recv, in_sem, send_sem, recv_sem,
+    rad_hbm, ion_hbm, dens_hbm, lum_hbm, cell_hbm, offset_hbm, count_hbm, final,
+    raw, lum, cell, offset, count, table, own, own_e, ions, flux_buf, strips,
+    y_send, d_send, x_recv, y_recv, d_recv, table_recv, in_sem, send_sem, recv_sem,
 ):
     nx, ny = lax.axis_size("gx"), lax.axis_size("gy")
     me_x, me_y = lax.axis_index("gx"), lax.axis_index("gy")
@@ -94,13 +94,13 @@
         pltpu.make_async_copy(src, dst, in_sem.at[i])
         for i, (src, dst) in enumerate(
             (
-                (rad_hbm, raw.at[pl.ds(0, FIELDS)]),
-                (ion_hbm, raw.at[ION]),
-                (dens_hbm, raw.at[DENS]),
                 (lum_hbm, lum),
                 (cell_hbm, cell),
                 (offset_hbm, offset),
                 (count_hbm, count),
+                (rad_hbm, raw.at[pl.ds(0, FIELDS)]),
+                (ion_hbm, raw.at[ION]),
+                (dens_hbm, raw.at[DENS]),
             )
         )
     ]
@@ -129,50 +129,66 @@
         copy.start()
         return copy
 
-    for copy in copies_in[:3]:
-        copy.wait()
-
-    for x in range(ROWS):
-        for a in range(STATE):
-            own[a, x + HALO] = raw[a, pl.ds(x, DEPTH, stride=ROWS), :]
-
-    for copy in copies_in[3:]:
+    for copy in copies_in[:4]:
         copy.wait()
     stars = lum.shape[1]
     live = (lax.broadcasted_iota(jnp.int32, (1, stars), 1) < count[...]).astype(F32)
-
-    def corner_weight(axis, position, wrapped=False):
-        low, frac = cell[axis], offset[axis]
-        high = low + 1
-        if wrapped:
-            high = jnp.where(high >= DEPTH, high - DEPTH, high)
-        return jnp.where(low == position, 1.0 - frac, 0.0) + jnp.where(high == position, frac, 0.0)
-
-    z_at = lax.broadcasted_iota(jnp.int32, (DEPTH, stars), 0)
-    weight_z = corner_weight(2, z_at, True)
-    strength = [weight_z * (lum[g : g + 1, :] * live * DT) for g in range(2)]
-    y_at = lax.broadcasted_iota(jnp.int32, (LANES, stars), 0)
-    weight_y = corner_weight(1, y_at)
-    weight_x = corner_weight(0, y_at)
-    over_y = corner_weight(1, jnp.full((1, stars), LANES, jnp.int32))
-    weight_rows = [corner_weight(0, jnp.full((1, stars), x, jnp.int32)) for x in range(ROWS + 1)]
-    spread = [strength[g] * weight_rows[x] for g in range(2) for x in range(ROWS + 1)]
+    for g in range(2):
+        table[g : g + 1, :] = lum[g : g + 1, :] * live * DT
+    for axis in range(3):
+        table[2 + axis : 3 + axis, :] = cell[axis].astype(F32)
+        table[5 + axis : 6 + axis, :] = offset[axis]
     contract = functools.partial(
         lax.dot_general,
         dimension_numbers=(((1,), (1,)), ((), ())),
         precision=lax.Precision.HIGHEST,
         preferred_element_type=F32,
     )
-    deposit = contract(jnp.concatenate(spread, axis=0), weight_y)
-    column = contract(jnp.concatenate([s * over_y for s in strength], axis=0), weight_x)
-    moved = [[None] * (ROWS + 1) for _ in range(2)]
+
+    def deposits(stars_at, rows):
+        def corner_weight(axis, position, wrapped=False):
+            low, frac = stars_at[2 + axis : 3 + axis, :], stars_at[5 + axis : 6 + axis, :]
+            high = low + 1.0
+            if wrapped:
+                high = jnp.where(high >= DEPTH, high - DEPTH, high)
+            return jnp.where(low == position, 1.0 - frac, 0.0) + jnp.where(high == position, frac, 0.0)
+
+        z_at = lax.broadcasted_iota(jnp.int32, (DEPTH, stars), 0).astype(F32)
+        y_at = lax.broadcasted_iota(jnp.int32, (LANES, stars), 0).astype(F32)
+        weight_z = corner_weight(2, z_at, True)
+        strength = [weight_z * stars_at[g : g + 1, :] for g in range(2)]
+        weight_rows = [corner_weight(0, jnp.full((1, stars), x, F32)) for x in rows]
+        spread = [strength[g] * weight for g in range(2) for weight in weight_rows]
+        over_y = corner_weight(1, jnp.full((1, stars), LANES, F32))
+        deposit = contract(jnp.concatenate(spread, axis=0), corner_weight(1, y_at))
+        column = contract(jnp.concatenate([s * over_y for s in strength], axis=0), corner_weight(0, y_at))
+        here, moved = [], []
+        for g in range(2):
+            for i, x in enumerate(rows):
+                at = (g * len(rows) + i) * DEPTH
+                row = deposit[at : at + DEPTH]
+                over = lane_roll(column[g * DEPTH : (g + 1) * DEPTH], LANES - 1 - x)
+                here.append(row)
+                moved.append(jnp.where(lane == LANES - 1, over, lane_roll(row, -1)))
+        return here, moved
+
+    def strip_of_deposit(row, moved, s, old):
+        at = STRIP * s
+        old = old + jnp.where(between(lane, at + 1, 8), lane_roll(moved, at + 9), 0.0)
+        return old + jnp.where(between(lane, at + 16, 8), lane_roll(row, at + 16), 0.0)
+
+    here, moved_rows = deposits(table, range(ROWS + 1))
+    moved = [moved_rows[: ROWS + 1], moved_rows[ROWS + 1 :]]
     for g in range(2):
         for x in range(ROWS + 1):
-            at = (g * (ROWS + 1) + x) * DEPTH
-            row = deposit[at : at + DEPTH]
-            own_e[g, HALO + x] = row
-            over = lane_roll(column[g * DEPTH : (g + 1) * DEPTH], LANES - 1 - x)
-            moved[g][x] = jnp.where(lane == LANES - 1, over, lane_roll(row, -1))
+            own_e[g, HALO + x] = here[g * (ROWS + 1) + x]
+
+    for copy in copies_in[4:]:
+        copy.wait()
+
+    for x in range(ROWS):
+        for a in range(STATE):
+            own[a, x + HALO] = raw[a, pl.ds(x, DEPTH, stride=ROWS), :]
 
     def array_row(a, r):
         return own[a, r] if a < STATE else own_e[a - STATE, r]
@@ -190,34 +206,13 @@
                 total = jnp.where(between(lane, base, 4), piece, total)
             y_send[side, a] = total
 
-    for g in range(2):
-        strip = []
-        for v in range(SLOTS):
-            total = zeros
-            for s in range(SLOTS):
-                x, at = SLOTS * s + v - HALO, STRIP * s
-                if 0 <= x <= ROWS:
-                    total = jnp.where(between(lane, at + 1, 8), lane_roll(moved[g][x], at + 9), total)
-                    total = jnp.where(between(lane, at + 16, 8), lane_roll(own_e[g, x + HALO], at + 16), total)
-            strip.append(total)
-            strips[STATE + g, v] = total
-        for i, (first, target) in enumerate(((ROWS + 1, 1), (HALO, ROWS + HALO))):
-            total = zeros
-            for j in range(HALO):
-                e_send[i, g, j] = own_e[g, first + j]
-                s, v = divmod(first + j, SLOTS)
-                place = (target + j) % SLOTS
-                piece = lane_roll(strip[v], STRIP * (place - s))
-                total = jnp.where(between(lane, STRIP * place, STRIP), piece, total)
-            e_send[i, g, HALO] = total
-
     pl.semaphore_wait(barrier, len(DIRS))
     y_copies = [send(y_send.at[i], y_recv.at[i], i, DIRS[i]) for i in range(2)]
+    table_copies = [send(table, table_recv.at[i], 4 + i, DIRS[2 + i]) for i in range(2)]
     x_copies = []
     for i in range(2):
         rows = own.at[:, pl.ds(HALO if i else ROWS, HALO)]
         x_copies.append(send(rows, x_recv.at[i], 2 + i, DIRS[2 + i]))
-        x_copies.append(send(e_send.at[i], e_recv.at[i], 4 + i, DIRS[2 + i]))
 
     def store_flux(k, g, r, u):
         here, to_lower, to_upper = fluxes(u)
@@ -244,6 +239,15 @@
                 final[i, r] = u[i]
             final[ION, r] = x
 
+    for g in range(2):
+        for v in range(SLOTS):
+            total = zeros
+            for s in range(SLOTS):
+                x = SLOTS * s + v - HALO
+                if 0 <= x <= ROWS:
+                    total = strip_of_deposit(own_e[g, x + HALO], moved[g][x], s, total)
+            strips[STATE + g, v] = total
+
     for r in range(HALO, HALO + ROWS):
         ions[0, r] = own[ION, r]
         ions[SUBSTEPS, r] = own[DENS, r]
@@ -301,6 +305,18 @@
         for v in range(SLOTS):
             strips[a, v] = add_edges(y_recv[0, a], y_recv[1, a], v, a >= STATE, strips[a, v], None)
 
+    for copy in table_copies:
+        copy.wait_recv()
+    for i, rows in enumerate((range(ROWS - HALO + 1, ROWS + 1), range(HALO - 1))):
+        from_x, from_x_moved = deposits(table_recv.at[i], rows)
+        for g in range(2):
+            for j, x in enumerate(rows):
+                r = x + HALO + (ROWS if i else -ROWS)
+                s, v = divmod(r, SLOTS)
+                row, row_moved = from_x[g * len(rows) + j], from_x_moved[g * len(rows) + j]
+                own_e[g, r] = row + own_e[g, r] if r in (HALO, ROWS + HALO) else row
+                strips[STATE + g, v] = strip_of_deposit(row, row_moved, s, strips[STATE + g, v])
+
     for copy in x_copies:
         copy.wait_recv()
     for j in range(HALO):
@@ -309,34 +325,12 @@
             ions[SUBSTEPS, r] = x_recv[i, DENS, j]
             for g in range(2):
                 store_flux(0, g, r, [x_recv[i, 4 * g + c, j] for c in range(4)])
-    for g in range(2):
-        for j in range(HALO):
-            low, high = 1 + j, ROWS + HALO + j
-            if j < HALO - 1:
-                own_e[g, low] = e_recv[0, g, j]
-            else:
-                own_e[g, low] = own_e[g, low] + e_recv[0, g, j]
-            if j == 0:
-                own_e[g, high] = own_e[g, high] + e_recv[1, g, j]
-            else:
-                own_e[g, high] = e_recv[1, g, j]
-    for k in range(1, SUBSTEPS + 1):
-        for i in range(HALO):
-            substep(k, k + i)
-            substep(k, ROWS + HALO - k + i)
 
     outer = (lane < STRIP) | between(lane, STRIP * (SLOTS - 1), STRIP)
     for a in range(STATE):
         for v in range(HALO):
             value = pack_strip(x_recv[0, a, v], 0, strips[a, v])
             strips[a, v] = pack_strip(x_recv[1, a, v], SLOTS - 1, value)
-    for g in range(2):
-        for v in range(SLOTS):
-            last = STRIP * (SLOTS - 1)
-            value = strips[STATE + g, v]
-            value = value + jnp.where(lane < STRIP, lane_roll(e_recv[0, g, HALO], -STRIP * v), 0.0)
-            piece = lane_roll(e_recv[1, g, HALO], last - STRIP * v)
-            strips[STATE + g, v] = value + jnp.where(between(lane, last, STRIP), piece, 0.0)
     for copy in d_copies:
         copy.wait_recv()
 
@@ -371,24 +365,34 @@
         for g in range(2):
             store_flux(0, g, STRIP_ROW + v, [strips[4 * g + c, v] for c in range(4)])
     for k in range(1, SUBSTEPS + 1):
+        for i in range(HALO):
+            substep(k, k + i)
+            substep(k, ROWS + HALO - k + i)
         wrap_strips(k - 1)
 
         for v in range(SLOTS):
             substep(k, STRIP_ROW + v)
 
-    for x in range(ROWS):
-        s, v = divmod(x + HALO, SLOTS)
-        for a in range(FIELDS + 1):
+    for copy in y_copies + table_copies + x_copies + d_copies:
+        copy.wait_send()
+
+
+def merge_kernel(final, rad_out, ion_out, raw_out, out_sem):
+    lane = lax.broadcasted_iota(jnp.int32, (DEPTH, LANES), 1)
+    copies = []
+    for a in range(FIELDS + 1):
+        for x in range(ROWS):
+            s, v = divmod(x + HALO, SLOTS)
             edge_cols = final[a, STRIP_ROW + v]
             value = final[a, x + HALO]
             value = jnp.where(lane < HALO, lane_roll(edge_cols, -16 - STRIP * s), value)
             value = jnp.where(lane >= LANES - HALO, lane_roll(edge_cols, -8 - STRIP * s), value)
-            if a < FIELDS:
-                rad_out[a, pl.ds(x, DEPTH, stride=ROWS), :] = value
-            else:
-                ion_out[pl.ds(x, DEPTH, stride=ROWS), :] = value
-    for copy in y_copies + x_copies + d_copies:
-        copy.wait_send()
+            raw_out[a, pl.ds(x, DEPTH, stride=ROWS), :] = value
+        target = rad_out.at[a] if a < FIELDS else ion_out
+        copies.append(pltpu.make_async_copy(raw_out.at[a], target, out_sem.at[a]))
+        copies[-1].start()
+    for copy in copies:
+        copy.wait()
 
 
 def on_device(radiation, ion_fraction, density, star_lum, star_cell, star_offset, star_count):
@@ -398,33 +402,29 @@
     plane = (depth * rows, lanes)
     vmem = lambda *shape: pltpu.VMEM(shape + (DEPTH, LANES), F32)
     hbm = lambda value: pltpu.with_memory_space_constraint(value, pltpu.HBM)
-    rad, ion = pl.pallas_call(
+    final = pl.pallas_call(
         kernel,
-        out_shape=(
-            jax.ShapeDtypeStruct((FIELDS,) + plane, F32),
-            jax.ShapeDtypeStruct(plane, F32),
-        ),
+        out_shape=jax.ShapeDtypeStruct((FIELDS + 1, TOTAL_ROWS, DEPTH, LANES), F32),
         in_specs=[pl.BlockSpec(memory_space=pltpu.HBM)] * 7,
-        out_specs=(pl.BlockSpec(memory_space=pltpu.VMEM),) * 2,
+        out_specs=pl.BlockSpec(memory_space=pltpu.VMEM),
         scratch_shapes=[
             pltpu.VMEM((STATE,) + plane, F32),
             pltpu.VMEM((2, stars), F32),
             pltpu.VMEM((3, 1, stars), jnp.int32),
             pltpu.VMEM((3, 1, stars), F32),
             pltpu.VMEM((1, 1), jnp.int32),
+            pltpu.VMEM((8, stars), F32),
             vmem(STATE, ROWS + 2 * HALO),
             vmem(2, TOTAL_ROWS),
             vmem(SUBSTEPS + 1, TOTAL_ROWS),
             vmem(SUBSTEPS, 2, 12, TOTAL_ROWS),
             vmem(ARRAYS, SLOTS),
-            vmem(FIELDS + 1, TOTAL_ROWS),
             vmem(2, ARRAYS),
             vmem(2, 2, 3),
-            vmem(2, 2, HALO + 1),
             vmem(2, STATE, HALO),
             vmem(2, ARRAYS),
             vmem(2, 2, 3),
-            vmem(2, 2, HALO + 1),
+            pltpu.VMEM((2, 8, stars), F32),
             pltpu.SemaphoreType.DMA((7,)),
             pltpu.SemaphoreType.DMA((8,)),
             pltpu.SemaphoreType.DMA((8,)),
@@ -441,6 +441,19 @@
         hbm(star_offset.reshape(3, 1, stars)),
         star_count,
     )
+    rad, ion = pl.pallas_call(
+        merge_kernel,
+        out_shape=(
+            jax.ShapeDtypeStruct((FIELDS,) + plane, F32),
+            jax.ShapeDtypeStruct(plane, F32),
+        ),
+        in_specs=[pl.BlockSpec(memory_space=pltpu.VMEM)],
+        out_specs=(pl.BlockSpec(memory_space=pltpu.HBM),) * 2,
+        scratch_shapes=[
+            pltpu.VMEM((FIELDS + 1,) + plane, F32),
+            pltpu.SemaphoreType.DMA((FIELDS + 1,)),
+        ],
+    )(pltpu.with_memory_space_constraint(final, pltpu.VMEM))
     return rad.reshape(radiation.shape), ion.reshape(ion_fraction.shape)
 
 

time: 25.3 us -> 23.8 us (0.941)
  local copies, waits for them, and re-layouts: 1.42 us -> 0 us
    unnamed x2 -> x0, local copies, waits for them, and re-layouts: 1.42 us -> none
    pallas_call x1 -> x2, Pallas kernels: 22.5 us -> 22.4 us  [the longest x1 21.4 us: on_device(): pl.pallas_call(kernel, out_shape=jax.ShapeDtypeStruct((FIELDS + 1, TOTAL_...]
where the time goes in v3:
time: 23.8 us; the launch traced here: 23.7 us
  Pallas kernels  22.4 us (94%)
  between operations  1.29 us (5%)
    pallas_call x1, Pallas kernels, on_device(): pl.pallas_call(kernel, out_shape=jax.ShapeDtypeStruct((FIELDS + 1, TOTAL_...  21.4 us
    pallas_call x1, Pallas kernels, on_device(): pl.pallas_call(merge_kernel, out_shape=(jax.ShapeDtypeStruct((FIELDS,) +...  1.08 us

profile of v3, /device:TPU:0, one launch (start us, length us, event | category | flops | bytes accessed | tf_op | source)
XLA Modules:
  0.0 23.7 jit_solution(848657791087352515)
XLA Ops:
  1.3 21.4 %shard_map.86.final = f32[9,31,8,128]{3,2,1,0:T(8,128)S(1)} custom-call(f32[8,128,128]{2,1,0:T(8,128)} %bitcast.8, f32[128,128]{1,0:T(8,128)} %bitcast.9, f32[128,128]{1,0:T(8,128)} %bitcast.10, f32[2,256]{1,0:T(2,128)} %bitcast.13, s32[3,1,256]{2,1,0:T(1,128)} %bitcast.11, f32[3,1,256]{2,1,0:T(1,128)} %bitcast.12, s32[1,1]{1,0:T(1,128)S(6)} %copy.9.count_hbm), custom_call_target="tpu_custom_call" | custom-call | tf_op jit(solution)/shard_map/pallas_call | solution.py:405
  22.6 1.1 %shard_map.87 = (f32[8,128,128]{2,1,0:T(8,128)}, f32[128,128]{1,0:T(8,128)}) custom-call(f32[9,31,8,128]{3,2,1,0:T(8,128)S(1)} %shard_map.86.final), custom_call_target="tpu_custom_call" | custom-call | tf_op jit(solution)/shard_map/pallas_call | solution.py:444
